TPU v7x, 128 devices: a whole 4x4x4 slice. The times are simulated.
128 devices in a mesh: expert: 8 (over y, z_lo), shard: 16 (over z_hi, x, core).
Axes of the slice: x: 4, y: 4, z: 4 (z_hi: 2, z_lo: 2; z = z_hi * 2 + z_lo), core: 2. Of those that a mesh axis runs over, the one named last changes fastest.
Arguments:
- pre_hidden: bfloat16 [7680, 4096], P(('expert', 'shard')), may hold values from -12 to 12
- dec_resid: bfloat16 [16, 32, 4096], P('shard', 'expert'), may hold values from -12 to 12
- dec_query: bfloat16 [512, 4096], P('shard', 'expert'), may hold values from -4.5 to 4.5
- kv_pool: bfloat16 [8, 16896, 16, 256], P('expert', 'shard'), may hold values from -4.5 to 4.5
- page_table: int32 [16, 32, 128], P('shard'), may hold values from 0 to 1055, as said below
- cache_len: int32 [16, 32], P('shard'), may hold values from 2 to 2048, as said below
- out_weight: bfloat16 [4096, 4096], P('expert'), may hold values from -0.5 to 0.5
- norm_gain: float32 [4096], replicated, may hold values from 0.5 to 1.5
- route_ids_pre: int32 [7680, 2], P(('expert', 'shard')), may hold values from 0 to 7, as said below
- route_ids_dec: int32 [16, 32, 2], P('shard', 'expert'), may hold values from 0 to 7, as said below
- route_logit_pre: float32 [7680, 2], P(('expert', 'shard')), may hold values from -6 to 6
- route_logit_dec: float32 [16, 32, 2], P('shard', 'expert'), may hold values from -6 to 6
- expert_slot: int32 [8], replicated, may hold values from 0 to 7, each once
- w_gate: bfloat16 [8, 4096, 8192], P('expert', None, 'shard'), may hold values from -0.09375 to 0.09375
- w_up: bfloat16 [8, 4096, 8192], P('expert', None, 'shard'), may hold values from -0.09375 to 0.09375
- w_down: bfloat16 [8, 8192, 4096], P('expert', 'shard'), may hold values from -0.0625 to 0.0625
Outputs:
- mixed_pre: bfloat16 [7680, 4096], P(('expert', 'shard'))
- mixed_dec: bfloat16 [16, 32, 4096], P('shard', 'expert')
Inputs may be any that keep to these rules, and one draw needn't show every extreme that they name: `cache_len`: the requests of one shard index hold at most 16384 cached positions together, and one of them holds exactly 2048. `page_table`: for request i of shard index s, entries j below ceil(cache_len[s, i] / 16) name pages of the pool of that shard index, all distinct over the shard index; the other entries are unused. `route_ids_pre`: each row names two different experts. The rows of one device (its 60 prefill rows and its 4 decode rows) name each expert at most 18 times, and some expert exactly 18 times on every device. `route_ids_dec`: as for route_ids_pre: a device's decode rows count with its prefill rows.
All inputs are finite; a program needn't handle non-finite values.
Results may differ from a plain program's by a relative error of at most 0.015.
Values may be sent and summed in bfloat16 or wider, within the bound.
A program may use at most 192 MiB of HBM per device.

v0:
```python
import jax
import jax.numpy as jnp
from jax import lax
from jax.sharding import PartitionSpec as P


def table_attention(dec_query, kv_pool, page_rows, lengths):
    dec_dev, local_cols = dec_query.shape
    kv_local, pool_dev, page_size, twice_dim = kv_pool.shape
    head_dim = twice_dim // 2
    group_size = local_cols // (head_dim * kv_local)
    span_tokens = page_rows.shape[1] * page_size
    queries = dec_query.reshape(dec_dev, kv_local, group_size, head_dim)
    gathered = kv_pool[:, page_rows].reshape(kv_local, dec_dev, span_tokens, twice_dim)
    scores = jnp.einsum(
        "rkgd,krtd->rkgt", queries, gathered[..., :head_dim], preferred_element_type=jnp.float32
    ) * head_dim ** (-0.5)
    live_pos = (jnp.arange(span_tokens, dtype=jnp.int32)[None, :] < lengths[:, None])[
        :, None, None, :
    ]
    row_top = jnp.max(jnp.where(live_pos, scores, -jnp.inf), axis=-1, keepdims=True)
    weights_f = jnp.where(live_pos, jnp.exp(scores - row_top), 0.0)
    totals = jnp.sum(weights_f, axis=-1)
    weights_b = weights_f.astype(jnp.bfloat16)
    summed = jnp.einsum(
        "rkgt,krtd->rkgd", weights_b, gathered[..., head_dim:], preferred_element_type=jnp.float32
    )
    return (summed / totals[..., None]).astype(jnp.bfloat16).reshape(dec_dev, local_cols)


def local(
    pre_hidden,
    dec_resid,
    dec_query,
    kv_pool,
    page_table,
    cache_len,
    out_weight,
    norm_gain,
    route_ids_pre,
    route_ids_dec,
    route_logit_pre,
    route_logit_dec,
    expert_slot,
    w_gate,
    w_up,
    w_down,
):
    n_expert = lax.axis_size("expert")
    page_rows = page_table[0]
    lengths = cache_len[0]
    attn = table_attention(dec_query, kv_pool, page_rows, lengths)
    head_total = lax.psum_scatter(
        jnp.dot(attn, out_weight, preferred_element_type=jnp.float32).astype(jnp.bfloat16),
        "expert",
        scatter_dimension=0,
        tiled=True,
    ).astype(jnp.float32)
    h_dec = (dec_resid[0].astype(jnp.float32) + head_total).astype(jnp.bfloat16)
    hidden = jnp.concatenate([pre_hidden, h_dec], axis=0)
    route_ids = jnp.concatenate([route_ids_pre, route_ids_dec[0]], axis=0)
    logits = jnp.concatenate([route_logit_pre, route_logit_dec[0]], axis=0)
    pre_count = pre_hidden.shape[0]
    rows_dev, width = hidden.shape
    slot_cap = (rows_dev + 3) // 4 + 2
    stream = hidden.astype(jnp.float32)
    normed = (
        stream * lax.rsqrt(jnp.mean(stream * stream, axis=-1, keepdims=True) + 1e-05) * norm_gain
    ).astype(jnp.bfloat16)
    shares = jnp.stack(
        [jax.nn.sigmoid(logits[:, 0] - logits[:, 1]), jax.nn.sigmoid(logits[:, 1] - logits[:, 0])],
        axis=-1,
    )
    experts = expert_slot.shape[0]
    per_group = w_gate.shape[0]
    expert_ids = jnp.arange(experts, dtype=jnp.int32)
    slot_match = expert_slot[None, :] == expert_ids[:, None]
    slot_of = jnp.sum(jnp.where(slot_match, expert_ids[None, :], 0), axis=1)
    slot_ids = jnp.sum(jnp.where(route_ids[..., None] == expert_ids, slot_of, 0), axis=-1)
    flat_slots = slot_ids.reshape(-1)
    slot_hot = (flat_slots[:, None] == expert_ids[None, :]).astype(jnp.int32)
    ranking = jnp.sum((jnp.cumsum(slot_hot, axis=0) - slot_hot) * slot_hot, axis=1)
    slot_pos = (flat_slots * slot_cap + ranking).reshape(rows_dev, 2)
    slots_all = experts * slot_cap
    placing = jnp.any(
        jnp.arange(slots_all, dtype=jnp.int32)[:, None, None] == slot_pos[None], axis=-1
    ).astype(jnp.bfloat16)
    buffer = jnp.dot(placing, normed, preferred_element_type=jnp.float32).astype(jnp.bfloat16)
    buffer = buffer.reshape(n_expert, per_group, slot_cap, width)
    received = lax.all_to_all(buffer, "expert", split_axis=0, concat_axis=0, tiled=True)
    piece_rows = lax.all_gather(received[None], "shard", axis=0, tiled=True)
    gate = jnp.einsum("sgkcd,kdf->sgkcf", piece_rows, w_gate, preferred_element_type=jnp.float32)
    upper = jnp.einsum("sgkcd,kdf->sgkcf", piece_rows, w_up, preferred_element_type=jnp.float32)
    act = (jax.nn.silu(gate) * upper).astype(jnp.bfloat16)
    term = jnp.einsum("sgkcf,kfd->sgkcd", act, w_down, preferred_element_type=jnp.float32)
    own_rows = lax.psum_scatter(
        term.astype(jnp.bfloat16).astype(jnp.float32).astype(jnp.bfloat16),
        "shard",
        scatter_dimension=0,
        tiled=True,
    ).astype(jnp.float32)
    outputs = own_rows[0].astype(jnp.bfloat16)
    returned = lax.all_to_all(outputs, "expert", split_axis=0, concat_axis=0, tiled=True).reshape(
        slots_all, width
    )
    picked = returned[slot_pos]
    mixed_rows = stream + jnp.sum(shares[..., None] * picked.astype(jnp.float32), axis=1)
    mixed_out = mixed_rows.astype(jnp.bfloat16)
    return (mixed_out[:pre_count], mixed_out[pre_count:][None])


def solution(mesh):
    placed = (
        P(("expert", "shard"), None),
        P("shard", "expert", None),
        P("shard", "expert"),
        P("expert", "shard", None, None),
        P("shard", None, None),
        P("shard", None),
        P("expert", None),
        P(),
        P(("expert", "shard"), None),
        P("shard", "expert", None),
        P(("expert", "shard"), None),
        P("shard", "expert", None),
        P(),
        P("expert", None, "shard"),
        P("expert", None, "shard"),
        P("expert", "shard", None),
    )
    return jax.shard_map(
        local,
        mesh=mesh,
        in_specs=placed,
        out_specs=(P(("expert", "shard"), None), P("shard", "expert", None)),
        check_vma=False,
    )
```

profile of v0, /device:TPU:0, one launch (start us, length us, event | category | flops | bytes accessed | tf_op | source)
XLA Modules:
  0.0 599.9 jit_solution(9120764802494427658)
XLA Ops:
  7.2 0.0 all-reduce.3.cloned.1.call-start
  7.2 0.7 fusion.44
  7.9 0.8 reshape.189
  8.7 0.8 iota_compare_fusion
  9.5 40.6 %gather_fusion = bf16[4096,16,256]{2,1,0:T(8,128)(2,1)} fusion(bf16[1056,16,256]{2,1,0:T(8,128)(2,1)} %bitcast.140, s32[4096]{0:T(1024)S(1)} %fusion.44), kind=kCustom, calls=%fused_computation | custom fusion | bytes 67125248 | tf_op jit(solution)/shard_map/gather | solution.py:14
  50.1 8.0 %fusion.24 = f32[32,2048,4]{1,2,0:T(4,128)S(1)} fusion(bf16[32,4,128]{2,1,0:T(4,128)(2,1)S(1)} %reshape.189, bf16[1,32,2048,256]{3,2,1,0:T(8,128)(2,1)} %bitcast.141), kind=kOutput, calls=%fused_computation.28 | convolution fusion | flops 67371008 | bytes 17858560 | tf_op jit(solution)/shard_map/rkgd,krtd->rkgt/dot_general | solution.py:15
  58.1 1.1 fusion.48
  59.2 0.0 copy-start.2
  59.2 0.0 copy-start.10
  59.2 0.0 copy-start.6
  59.2 0.0 copy-start.7
  59.2 0.0 copy-start.11
  59.3 0.0 copy-start.4
  59.3 0.0 copy-start.1
  59.3 0.0 copy-start.5
  59.3 7.2 %fusion.27 = bf16[32,4,128]{2,1,0:T(4,128)(2,1)S(1)} fusion(bf16[1,32,2048,256]{3,2,1,0:T(8,128)(2,1)} %bitcast.142, bf16[32,4,2048]{2,1,0:T(4,128)(2,1)S(1)} %get-tuple-element.5, f32[32,4]{1,0:T(8,128)S(1)} %get-tuple-element.4), kind=kOutput, calls=%fused_computation.36 | convolution fusion | flops 67141632 | bytes 17334784 | tf_op jit(solution)/shard_map/rkgt,krtd->rkgd/dot_general | solution.py:25
  66.5 1.5 convolution_convert_fusion.1
  68.0 0.0 all-reduce.3.cloned.1.call-update
  68.1 0.0 all-gather.3.cloned.1.call-start
  68.1 0.1 select_reduce_fusion.3
  68.3 0.1 pad_add_fusion
  68.3 0.1 select_reduce_fusion.2
  68.4 0.1 copy.38
  68.5 0.1 eq.61
  68.7 0.1 fusion.40
  68.8 0.2 reduce_window_sum.11
  68.9 0.2 select_reduce_fusion.1
  69.1 0.1 reduce_sum.62
  69.3 0.1 copy.39
  69.3 0.6 dynamic-slice
  70.6 0.1 fusion.38
  70.7 73.8 %all-reduce.3.cloned.1.call-done = bf16[32,4096]{1,0:T(8,128)(2,1)} async-done(((bf16[32,4096]{1,0:T(8,128)(2,1)}), bf16[32,4096]{1,0:T(8,128)(2,1)}) %all-reduce.3.cloned.1.call-update) | async-done | bytes 262160
  144.5 0.9 fusion.39
  145.4 0.2 fusion.28
  145.6 0.5 convolution_convert_fusion
  146.1 0.4 reshape.192
  146.6 18.4 %all_to_all.10 = bf16[8,1,18,4096]{3,2,1,0:T(8,128)(2,1)S(1)} all-to-all(bf16[8,1,18,4096]{3,2,1,0:T(8,128)(2,1)S(1)} %bitcast.145), channel_id=1, replica_groups=mesh['expert'=8,'shard'=16] {'expert'}, dimensions={0} | all-to-all | bytes 2359296 | tf_op jit(solution)/shard_map/all_to_all | solution.py:90
  165.0 1.7 copy.41
  166.7 0.0 all-gather.3.cloned.1.call-update
  166.7 0.2 reduce-scatter.2.cloned.1.call-start
  166.9 119.6 %all-gather.3.cloned.1.call-done = bf16[128,1,18,4096]{3,0,2,1:T(8,128)(2,1)} async-done(((bf16[8,1,18,4096]{3,0,2,1:T(8,128)(2,1)}), bf16[128,1,18,4096]{3,0,2,1:T(8,128)(2,1)}) %all-gather.3.cloned.1.call-update) | async-done | bytes 18874384 | tf_op jit(solution)/shard_map/all_gather | solution.py:91
  286.6 16.0 %copy.42 = bf16[128,1,18,4096]{3,2,0,1:T(8,128)(2,1)S(1)} copy(bf16[128,1,18,4096]{3,0,2,1:T(8,128)(2,1)} %all-gather.3.cloned.1.call-done) | data formatting | bytes 37748736 | tf_op jit(solution)/shard_map/all_gather | solution.py:91
  302.6 8.3 %copy-done = bf16[128,1,18,4096]{3,2,0,1:T(8,128)(2,1)} copy-done((bf16[128,1,18,4096]{3,2,0,1:T(8,128)(2,1)}, bf16[128,1,18,4096]{3,2,0,1:T(8,128)(2,1)S(1)}, u32[]{:S(2)}) %copy-start) | copy-done | bytes 18874392
  310.9 17.8 %fusion.12 = f32[16,8,18,512]{3,2,1,0:T(8,128)} fusion(bf16[16,8,18,4096]{3,2,1,0:T(8,128)(2,1)S(1)} %bitcast.143, bf16[1,4096,512]{2,1,0:T(8,128)(2,1)} %param.29), kind=kOutput, calls=%fused_computation.20 | convolution fusion | flops 9663676416 | bytes 27787264 | tf_op jit(solution)/shard_map/sgkcd,kdf->sgkcf/dot_general | solution.py:92
  328.7 19.8 %fusion.64 = bf16[16,8,18,512]{3,2,1,0:T(8,128)(2,1)} fusion(bf16[16,8,18,4096]{3,2,1,0:T(8,128)(2,1)} %bitcast.144, bf16[1,4096,512]{2,1,0:T(8,128)(2,1)} %param.30, f32[16,8,18,512]{3,2,1,0:T(8,128)} %fusion.12), kind=kOutput, calls=%fused_computation.22.clone.1 | convolution fusion | flops 9670754304 | bytes 30146560 | tf_op jit(solution)/shard_map/sgkcd,kdf->sgkcf/dot_general | solution.py:93
  348.4 20.6 %convert_bitcast_fusion = bf16[16,8,1,18,4096]{4,3,1,0,2:T(8,128)(2,1)} fusion(bf16[1,512,4096]{2,1,0:T(8,128)(2,1)} %param.31, bf16[16,8,18,512]{3,2,1,0:T(8,128)(2,1)} %fusion.64), kind=kOutput, calls=%fused_computation.3 | convolution fusion | flops 9673113600 | bytes 25427968 | tf_op jit(solution)/shard_map/sgkcf,kfd->sgkcd/dot_general | solution.py:95
  369.0 0.0 reduce-scatter.2.cloned.1.call-update
  369.0 188.4 %reduce-scatter.2.cloned.1.call-done = bf16[1,8,1,18,4096]{4,3,1,0,2:T(8,128)(2,1)} async-done(((bf16[16,8,1,18,4096]{4,3,1,0,2:T(8,128)(2,1)}), bf16[1,8,1,18,4096]{4,3,1,0,2:T(8,128)(2,1)}) %reduce-scatter.2.cloned.1.call-update) | async-done | bytes 1179664 | tf_op jit(solution)/shard_map/reduce_scatter | solution.py:96
  557.4 4.4 all-to-all-start.1
  561.8 0.1 reduce_sum.64
  561.9 0.1 copy.44
  562.0 0.1 copy.45
  562.1 0.2 reshape.212
  562.3 0.1 pad_maximum_fusion.2
  562.4 0.1 copy.37
  562.5 21.8 %all-to-all-done.1 = bf16[8,1,18,4096]{3,2,1,0:T(8,128)(2,1)S(1)} async-done(((bf16[8,1,18,4096]{3,2,1,0:T(8,128)(2,1)}), bf16[8,1,18,4096]{3,2,1,0:T(8,128)(2,1)S(1)}, u32[]{:S(2)}, u32[]{:S(2)}) %all-to-all-start.1) | async-done | bytes 1179680 | tf_op jit(solution)/shard_map/all_to_all | solution.py:103
  584.3 0.4 reshape.198
  584.7 2.2 gather_fusion.1
  586.9 2.4 reshape.224
  589.3 3.1 multiply_reduce_fusion
  592.4 0.1 fusion.31
  592.6 0.0 copy-start.3
  592.6 0.7 slice_bitcast_fusion.10
  593.3 0.1 copy-done.3
  (19 shorter events, 0.1 us)
Async XLA Ops:
  7.2 137.3 %all-reduce.3.cloned.1.call-start = ((), (), s32[]{:S(2)}) async-start(), calls=%async_computation.5 | async-start | bytes 524288
  59.2 7.3 %copy-start.2 = (bf16[512,4096]{1,0:T(8,128)(2,1)S(1)}, bf16[512,4096]{1,0:T(8,128)(2,1)}, u32[]{:S(2)}) copy-start(bf16[512,4096]{1,0:T(8,128)(2,1)} %param.22) | copy-start | bytes 12582916
  59.2 8.9 %copy-start.10 = (s32[8]{0:T(128)S(1)}, s32[8]{0:T(128)}, u32[]{:S(2)}) copy-start(s32[8]{0:T(128)} %param.28) | copy-start | bytes 100
  59.2 9.0 %copy-start.6 = (s32[1,4,2]{1,2,0:T(2,128)S(1)}, s32[1,4,2]{1,2,0:T(2,128)}, u32[]{:S(2)}) copy-start(s32[1,4,2]{1,2,0:T(2,128)} %param.25) | copy-start | bytes 100
  59.2 9.0 %copy-start.7 = (s32[60,2]{0,1:T(2,128)S(1)}, s32[60,2]{0,1:T(2,128)}, u32[]{:S(2)}) copy-start(s32[60,2]{0,1:T(2,128)} %param.24) | copy-start | bytes 1444
  59.2 10.1 %copy-start.11 = (u32[128]{0:T(128)S(1)}, u32[128]{0:T(128)}, u32[]{:S(2)}) copy-start(u32[128]{0:T(128)} %constant.45) | copy-start | bytes 1540
  59.3 85.2 %copy-start.4 = (bf16[1,4,4096]{2,1,0:T(4,128)(2,1)S(1)}, bf16[1,4,4096]{2,1,0:T(4,128)(2,1)}, u32[]{:S(2)}) copy-start(bf16[1,4,4096]{2,1,0:T(4,128)(2,1)} %param.17) | copy-start | bytes 98308
  59.3 86.1 %copy-start.1 = (bf16[60,4096]{1,0:T(8,128)(2,1)S(1)}, bf16[60,4096]{1,0:T(8,128)(2,1)}, u32[]{:S(2)}) copy-start(bf16[60,4096]{1,0:T(8,128)(2,1)} %param.16) | copy-start | bytes 1474564
  59.3 86.3 %copy-start.5 = (f32[4096]{0:T(1024)S(1)}, f32[4096]{0:T(1024)}, u32[]{:S(2)}) copy-start(f32[4096]{0:T(1024)} %param.23) | copy-start | bytes 49156
  68.1 218.5 %all-gather.3.cloned.1.call-start = ((), (), s32[]{:S(2)}) async-start(), calls=%async_computation.4 | async-start | bytes 20054016 | tf_op jit(solution)/shard_map/all_gather | solution.py:91
  166.7 390.7 %reduce-scatter.2.cloned.1.call-start = ((), (), s32[]{:S(2)}) async-start(), calls=%async_computation.3 | async-start | bytes 26738688 | tf_op jit(solution)/shard_map/reduce_scatter | solution.py:96
  302.6 8.3 %copy-start = (bf16[128,1,18,4096]{3,2,0,1:T(8,128)(2,1)}, bf16[128,1,18,4096]{3,2,0,1:T(8,128)(2,1)S(1)}, u32[]{:S(2)}) copy-start(bf16[128,1,18,4096]{3,2,0,1:T(8,128)(2,1)S(1)} %copy.42) | copy-start | bytes 56623108
  369.0 193.3 %copy-start.8 = (f32[1,4,2]{1,2,0:T(2,128)S(1)}, f32[1,4,2]{1,2,0:T(2,128)}, u32[]{:S(2)}) copy-start(f32[1,4,2]{1,2,0:T(2,128)} %param.27) | copy-start | bytes 100
  369.0 193.3 %copy-start.9 = (f32[60,2]{0,1:T(2,128)S(1)}, f32[60,2]{0,1:T(2,128)}, u32[]{:S(2)}) copy-start(f32[60,2]{0,1:T(2,128)} %param.26) | copy-start | bytes 1444
  557.4 26.9 %all-to-all-start.1 = ((bf16[8,1,18,4096]{3,2,1,0:T(8,128)(2,1)}), bf16[8,1,18,4096]{3,2,1,0:T(8,128)(2,1)S(1)}, u32[]{:S(2)}, u32[]{:S(2)}) async-start(bf16[8,1,18,4096]{3,2,1,0:T(8,128)(2,1)} %bitcast.146), calls=%async_computation.2 | async-start | bytes 3145728 | tf_op jit(solution)/shard_map/all_to_all | solution.py:103
  592.6 0.8 copy-start.3
Sparse Core Ops, SparseCore 0:
  68.2 76.2 all-reduce.2
  166.8 119.6 all-gather.2
  369.2 188.1 reduce-scatter.1
where the time goes:
time: 601 us; the launch traced here: 600 us
  waiting for transfers between devices  404 us (67%)
  matrix products  75.5 us (13%)
  local copies, waits for them, and re-layouts  75.2 us (13%)
  blocking collectives  18.4 us (3%)
  between operations  14.7 us (2%)
  other arithmetic  7.84 us (1%)
    reduce_scatter x1, waiting for transfers between devices, local(): lax.psum_scatter(term.astype(jnp.bfloat16).astype(jnp.float32).astype(jnp...  188 us
    all_gather x1, waiting for transfers between devices, local(): piece_rows = lax.all_gather(received[None], 'shard', axis=0, tiled=True)  120 us
    unnamed x4, waiting for transfers between devices  73.8 us
    gather x1, local copies, waits for them, and re-layouts, table_attention(): kv_pool[:, page_rows].reshape(kv_local, dec_dev, span_tokens, twice_dim)  40.6 us
    all_to_all x1, waiting for transfers between devices, local(): lax.all_to_all(outputs, 'expert', split_axis=0, concat_axis=0, tiled=True)  21.8 us
    dot_general x1, matrix products, local(): jnp.einsum('sgkcf,kfd->sgkcd', act, w_down, preferred_element_type=jnp.fl...  20.6 us
    dot_general x1, matrix products, local(): jnp.einsum('sgkcd,kdf->sgkcf', piece_rows, w_up, preferred_element_type=j...  19.8 us
    all_to_all x1, blocking collectives, local(): lax.all_to_all(buffer, 'expert', split_axis=0, concat_axis=0, tiled=True)  18.4 us
  transfers between devices with their start and end apart: 4, of which 4 were waited for; matrix products, arithmetic and copies ran while one was open for 0% of the time, Pallas kernels for 0%

commit v1 on v0

--- a/solution.py
+++ b/solution.py
@@ -88,7 +88,11 @@
     buffer = jnp.dot(placing, normed, preferred_element_type=jnp.float32).astype(jnp.bfloat16)
     buffer = buffer.reshape(n_expert, per_group, slot_cap, width)
     received = lax.all_to_all(buffer, "expert", split_axis=0, concat_axis=0, tiled=True)
-    piece_rows = lax.all_gather(received[None], "shard", axis=0, tiled=True)
+    x = received[None]
+    count = lax.axis_size("shard")
+    blocks = jnp.stack([x for _ in range(count)])
+    blocks = lax.all_to_all(blocks, "shard", split_axis=0, concat_axis=0)
+    piece_rows = jnp.concatenate(blocks, axis=0)
     gate = jnp.einsum("sgkcd,kdf->sgkcf", piece_rows, w_gate, preferred_element_type=jnp.float32)
     upper = jnp.einsum("sgkcd,kdf->sgkcf", piece_rows, w_up, preferred_element_type=jnp.float32)
     act = (jax.nn.silu(gate) * upper).astype(jnp.bfloat16)

time: 601 us -> 695 us (1.16)
  blocking collectives: 18.4 us -> 235 us
  waiting for transfers between devices: 404 us -> 282 us
  local copies, waits for them, and re-layouts: 75.2 us -> 52.1 us
  matrix products: 75.5 us -> 92.7 us
    all_to_all x0 -> x1, blocking collectives: none -> 217 us  [local(): blocks = lax.all_to_all(blocks, 'shard', split_axis=0, concat_axis=0)]
    all_gather x1 -> x0, waiting for transfers between devices: 120 us -> none  [local(): piece_rows = lax.all_gather(received[None], 'shard', axis=0, tiled=True)]
    all_gather x1 -> x0, local copies, waits for them, and re-layouts: 16 us -> none  [local(): piece_rows = lax.all_gather(received[None], 'shard', axis=0, tiled=True)]
    dot_general x1, matrix products: 19.8 us -> 29 us  [local(): jnp.einsum('sgkcd,kdf->sgkcf', piece_rows, w_up, preferred_element_type=j...]
    unnamed x25, local copies, waits for them, and re-layouts: 9.04 us -> 0.75 us
    dot_general x1, matrix products: 17.8 us -> 25.6 us  [local(): jnp.einsum('sgkcd,kdf->sgkcf', piece_rows, w_gate, preferred_element_type...]
    unnamed x4 -> x3, waiting for transfers between devices: 73.8 us -> 73.8 us
  transfers between devices with their start and end apart: 4 -> 3, of which waited for: 4 -> 3; matrix products, arithmetic and copies ran while one was open for 0% -> 0% of each run, Pallas kernels for 0% -> 0%
where the time goes in v1:
time: 695 us; the launch traced here: 689 us
  waiting for transfers between devices  282 us (41%)
  blocking collectives  235 us (34%)
  matrix products  92.7 us (13%)
  local copies, waits for them, and re-layouts  52.1 us (7%)
  between operations  15.2 us (2%)
  other arithmetic  7.84 us (1%)
    all_to_all x1, blocking collectives, local(): blocks = lax.all_to_all(blocks, 'shard', split_axis=0, concat_axis=0)  217 us
    reduce_scatter x1, waiting for transfers between devices, local(): lax.psum_scatter(term.astype(jnp.bfloat16).astype(jnp.float32).astype(jnp...  186 us
    unnamed x3, waiting for transfers between devices  73.8 us
    gather x1, local copies, waits for them, and re-layouts, table_attention(): kv_pool[:, page_rows].reshape(kv_local, dec_dev, span_tokens, twice_dim)  40.6 us
    dot_general x1, matrix products, local(): jnp.einsum('sgkcd,kdf->sgkcf', piece_rows, w_up, preferred_element_type=j...  29 us
    dot_general x1, matrix products, local(): jnp.einsum('sgkcd,kdf->sgkcf', piece_rows, w_gate, preferred_element_type...  25.6 us
    all_to_all x1, waiting for transfers between devices, local(): lax.all_to_all(outputs, 'expert', split_axis=0, concat_axis=0, tiled=True)  21.9 us
    dot_general x1, matrix products, local(): jnp.einsum('sgkcf,kfd->sgkcd', act, w_down, preferred_element_type=jnp.fl...  20.8 us
  transfers between devices with their start and end apart: 3, of which 3 were waited for; matrix products, arithmetic and copies ran while one was open for 0% of the time, Pallas kernels for 0%

profile of v1, /device:TPU:0, one launch (start us, length us, event | category | flops | bytes accessed | tf_op | source)
XLA Modules:
  0.0 688.9 jit_solution(17751042772438278228)
XLA Ops:
  7.2 0.0 all-reduce.3.cloned.1.call-start
  7.2 0.7 fusion.54
  7.9 0.8 reshape.195
  8.7 0.8 iota_compare_fusion
  9.5 40.6 %gather_fusion = bf16[4096,16,256]{2,1,0:T(8,128)(2,1)} fusion(bf16[1056,16,256]{2,1,0:T(8,128)(2,1)} %bitcast.149, s32[4096]{0:T(1024)S(1)} %fusion.54), kind=kCustom, calls=%fused_computation | custom fusion | bytes 67125248 | tf_op jit(solution)/shard_map/gather | solution.py:14
  50.1 8.0 %fusion.34 = f32[32,2048,4]{1,2,0:T(4,128)S(1)} fusion(bf16[32,4,128]{2,1,0:T(4,128)(2,1)S(1)} %reshape.195, bf16[1,32,2048,256]{3,2,1,0:T(8,128)(2,1)} %bitcast.150), kind=kOutput, calls=%fused_computation.32 | convolution fusion | flops 67371008 | bytes 17858560 | tf_op jit(solution)/shard_map/rkgd,krtd->rkgt/dot_general | solution.py:15
  58.1 1.1 fusion.58
  59.2 0.0 copy-start.1
  59.2 0.0 copy-start.10
  59.2 0.0 copy-start.5
  59.2 0.0 copy-start.6
  59.2 0.0 copy-start.11
  59.3 0.0 copy-start.3
  59.3 0.0 copy-start
  59.3 0.0 copy-start.4
  59.3 7.2 %fusion.37 = bf16[32,4,128]{2,1,0:T(4,128)(2,1)S(1)} fusion(bf16[1,32,2048,256]{3,2,1,0:T(8,128)(2,1)} %bitcast.151, bf16[32,4,2048]{2,1,0:T(4,128)(2,1)S(1)} %get-tuple-element.5, f32[32,4]{1,0:T(8,128)S(1)} %get-tuple-element.4), kind=kOutput, calls=%fused_computation.40 | convolution fusion | flops 67141632 | bytes 17334784 | tf_op jit(solution)/shard_map/rkgt,krtd->rkgd/dot_general | solution.py:25
  66.5 1.5 convolution_convert_fusion.1
  68.0 0.0 all-reduce.3.cloned.1.call-update
  68.1 0.0 reduce-scatter.2.cloned.1.call-start
  68.1 0.1 select_reduce_fusion.3
  68.2 0.1 pad_add_fusion
  68.3 0.1 select_reduce_fusion.2
  68.4 0.1 copy.38
  68.5 0.1 eq.61
  68.7 0.1 fusion.50
  68.7 0.2 reduce_window_sum.11
  68.9 0.2 select_reduce_fusion.1
  69.1 0.1 reduce_sum.62
  69.2 0.1 copy.39
  69.3 0.0 copy-done.11
  69.3 0.6 dynamic-slice
  70.6 0.1 fusion.48
  70.7 73.8 %all-reduce.3.cloned.1.call-done = bf16[32,4096]{1,0:T(8,128)(2,1)} async-done(((bf16[32,4096]{1,0:T(8,128)(2,1)}), bf16[32,4096]{1,0:T(8,128)(2,1)}) %all-reduce.3.cloned.1.call-update) | async-done | bytes 262160
  144.5 0.9 fusion.49
  145.3 0.0 copy-done
  145.3 0.2 fusion.38
  145.6 0.5 convolution_convert_fusion
  146.1 0.4 reshape.198
  146.6 18.4 %all_to_all.18 = bf16[8,1,18,4096]{3,2,1,0:T(8,128)(2,1)S(1)} all-to-all(bf16[8,1,18,4096]{3,2,1,0:T(8,128)(2,1)S(1)} %bitcast.152), channel_id=1, replica_groups=mesh['expert'=8,'shard'=16] {'expert'}, dimensions={0} | all-to-all | bytes 2359296 | tf_op jit(solution)/shard_map/all_to_all | solution.py:90
  165.0 0.7 copy.41
  165.6 2.2 stack.9
  167.9 0.0 copy-start.9
  167.9 216.6 %all_to_all.19 = bf16[16,1,8,1,18,4096]{5,2,4,3,1,0:T(8,128)(2,1)} all-to-all(bf16[16,1,8,1,18,4096]{5,2,4,3,1,0:T(8,128)(2,1)S(1)} %stack.9), channel_id=1, replica_groups=mesh['expert'=8,'shard'=16] {'shard'}, dimensions={0} | all-to-all | bytes 37748736 | tf_op jit(solution)/shard_map/all_to_all | solution.py:94
  384.5 25.6 %fusion.3 = f32[16,8,18,512]{3,2,1,0:T(8,128)} fusion(bf16[16,1,8,1,18,4096]{5,2,4,3,1,0:T(8,128)(2,1)} %all_to_all.19, bf16[1,4096,512]{2,1,0:T(8,128)(2,1)S(1)} %copy-done.9), kind=kOutput, calls=%fused_computation.5 | convolution fusion | flops 9663676416 | bytes 27787264 | tf_op jit(solution)/shard_map/sgkcd,kdf->sgkcf/dot_general | solution.py:96
  410.1 29.0 %fusion.72 = bf16[16,8,18,512]{3,2,1,0:T(8,128)(2,1)} fusion(bf16[1,4096,512]{2,1,0:T(8,128)(2,1)} %param.30, bf16[16,1,8,1,18,4096]{5,2,4,3,1,0:T(8,128)(2,1)} %all_to_all.19, f32[16,8,18,512]{3,2,1,0:T(8,128)} %fusion.3), kind=kOutput, calls=%fused_computation.26.clone.1 | convolution fusion | flops 9670754304 | bytes 30146560 | tf_op jit(solution)/shard_map/sgkcd,kdf->sgkcf/dot_general | solution.py:97
  439.1 20.8 %convert_bitcast_fusion = bf16[16,8,1,18,4096]{4,3,1,0,2:T(8,128)(2,1)} fusion(bf16[1,512,4096]{2,1,0:T(8,128)(2,1)} %param.31, bf16[16,8,18,512]{3,2,1,0:T(8,128)(2,1)} %fusion.72), kind=kOutput, calls=%fused_computation.9 | convolution fusion | flops 9673113600 | bytes 25427968 | tf_op jit(solution)/shard_map/sgkcf,kfd->sgkcd/dot_general | solution.py:99
  459.9 0.0 reduce-scatter.2.cloned.1.call-update
  459.9 185.9 %reduce-scatter.2.cloned.1.call-done = bf16[1,8,1,18,4096]{4,3,1,0,2:T(8,128)(2,1)} async-done(((bf16[16,8,1,18,4096]{4,3,1,0,2:T(8,128)(2,1)}), bf16[1,8,1,18,4096]{4,3,1,0,2:T(8,128)(2,1)}) %reduce-scatter.2.cloned.1.call-update) | async-done | bytes 1179664 | tf_op jit(solution)/shard_map/reduce_scatter | solution.py:100
  645.8 4.4 all-to-all-start.2
  650.2 0.1 reduce_sum.64
  650.3 0.1 copy.44
  650.4 0.1 copy.45
  650.5 0.2 reshape.218
  650.7 0.1 pad_maximum_fusion.2
  650.8 0.1 copy.37
  650.9 21.9 %all-to-all-done.2 = bf16[8,1,18,4096]{3,2,1,0:T(8,128)(2,1)S(1)} async-done(((bf16[8,1,18,4096]{3,2,1,0:T(8,128)(2,1)}), bf16[8,1,18,4096]{3,2,1,0:T(8,128)(2,1)S(1)}, u32[]{:S(2)}, u32[]{:S(2)}) %all-to-all-start.2) | async-done | bytes 1179680 | tf_op jit(solution)/shard_map/all_to_all | solution.py:107
  672.8 0.4 reshape.204
  673.2 2.2 gather_fusion.1
  675.4 2.4 reshape.228
  677.7 3.1 multiply_reduce_fusion
  680.9 0.1 fusion.41
  681.0 0.0 copy-start.2
  681.0 0.7 slice_bitcast_fusion.10
  681.7 0.1 copy-done.2
  (17 shorter events, 0.1 us)
Async XLA Ops:
  7.2 137.3 %all-reduce.3.cloned.1.call-start = ((), (), s32[]{:S(2)}) async-start(), calls=%async_computation.5 | async-start | bytes 524288
  59.2 7.3 %copy-start.1 = (bf16[512,4096]{1,0:T(8,128)(2,1)S(1)}, bf16[512,4096]{1,0:T(8,128)(2,1)}, u32[]{:S(2)}) copy-start(bf16[512,4096]{1,0:T(8,128)(2,1)} %param.22) | copy-start | bytes 12582916
  59.2 8.9 %copy-start.10 = (s32[8]{0:T(128)S(1)}, s32[8]{0:T(128)}, u32[]{:S(2)}) copy-start(s32[8]{0:T(128)} %param.28) | copy-start | bytes 100
  59.2 9.0 %copy-start.5 = (s32[1,4,2]{1,2,0:T(2,128)S(1)}, s32[1,4,2]{1,2,0:T(2,128)}, u32[]{:S(2)}) copy-start(s32[1,4,2]{1,2,0:T(2,128)} %param.25) | copy-start | bytes 100
  59.2 9.0 %copy-start.6 = (s32[60,2]{0,1:T(2,128)S(1)}, s32[60,2]{0,1:T(2,128)}, u32[]{:S(2)}) copy-start(s32[60,2]{0,1:T(2,128)} %param.24) | copy-start | bytes 1444
  59.2 10.1 %copy-start.11 = (u32[128]{0:T(128)S(1)}, u32[128]{0:T(128)}, u32[]{:S(2)}) copy-start(u32[128]{0:T(128)} %constant.45) | copy-start | bytes 1540
  59.3 85.2 %copy-start.3 = (bf16[1,4,4096]{2,1,0:T(4,128)(2,1)S(1)}, bf16[1,4,4096]{2,1,0:T(4,128)(2,1)}, u32[]{:S(2)}) copy-start(bf16[1,4,4096]{2,1,0:T(4,128)(2,1)} %param.17) | copy-start | bytes 98308
  59.3 86.1 %copy-start = (bf16[60,4096]{1,0:T(8,128)(2,1)S(1)}, bf16[60,4096]{1,0:T(8,128)(2,1)}, u32[]{:S(2)}) copy-start(bf16[60,4096]{1,0:T(8,128)(2,1)} %param.16) | copy-start | bytes 1474564
  59.3 86.3 %copy-start.4 = (f32[4096]{0:T(1024)S(1)}, f32[4096]{0:T(1024)}, u32[]{:S(2)}) copy-start(f32[4096]{0:T(1024)} %param.23) | copy-start | bytes 49156
  68.1 577.8 %reduce-scatter.2.cloned.1.call-start = ((), (), s32[]{:S(2)}) async-start(), calls=%async_computation.4 | async-start | bytes 26738688 | tf_op jit(solution)/shard_map/reduce_scatter | solution.py:100
  167.9 216.6 %copy-start.9 = (bf16[1,4096,512]{2,1,0:T(8,128)(2,1)S(1)}, bf16[1,4096,512]{2,1,0:T(8,128)(2,1)}, u32[]{:S(2)}) copy-start(bf16[1,4096,512]{2,1,0:T(8,128)(2,1)} %param.29) | copy-start | bytes 12582916
  459.9 190.8 %copy-start.7 = (f32[1,4,2]{1,2,0:T(2,128)S(1)}, f32[1,4,2]{1,2,0:T(2,128)}, u32[]{:S(2)}) copy-start(f32[1,4,2]{1,2,0:T(2,128)} %param.27) | copy-start | bytes 100
  459.9 190.8 %copy-start.8 = (f32[60,2]{0,1:T(2,128)S(1)}, f32[60,2]{0,1:T(2,128)}, u32[]{:S(2)}) copy-start(f32[60,2]{0,1:T(2,128)} %param.26) | copy-start | bytes 1444
  645.8 26.9 %all-to-all-start.2 = ((bf16[8,1,18,4096]{3,2,1,0:T(8,128)(2,1)}), bf16[8,1,18,4096]{3,2,1,0:T(8,128)(2,1)S(1)}, u32[]{:S(2)}, u32[]{:S(2)}) async-start(bf16[8,1,18,4096]{3,2,1,0:T(8,128)(2,1)} %bitcast.154), calls=%async_computation.3 | async-start | bytes 3145728 | tf_op jit(solution)/shard_map/all_to_all | solution.py:107
  681.0 0.8 copy-start.2
Sparse Core Ops, SparseCore 0:
  68.2 76.2 all-reduce.2
  460.0 185.7 reduce-scatter.1
